TPU v7x, 256 devices: a whole 4x4x8 slice. The times are simulated.
256 devices in a mesh: frame: 16 (over x_hi, z), head: 8 (over y, core), dp: 2 (over x_lo).
Axes of the slice: x: 4 (x_hi: 2, x_lo: 2; x = x_hi * 2 + x_lo), y: 4, z: 8, core: 2. Of those that a mesh axis runs over, the one named last changes fastest.
Arguments:
- clip: bfloat16 [2, 4096, 256], P('dp', 'frame'), may hold values from -40 to 40
- block_ids: int32 [2, 4096], P('dp'), may hold values from 0 to 63, never falling along the last dimension, each value on 1 to 128 neighbouring positions
- w_spatial: bfloat16 [9, 256, 256], replicated, may hold values from -0.125 to 0.125
- w_temporal: bfloat16 [3, 256, 256], replicated, may hold values from -0.21875 to 0.21875
- w_query: bfloat16 [256, 2048], P(None, 'head'), may hold values from -0.375 to 0.375
- w_key: bfloat16 [256, 2048], P(None, 'head'), may hold values from -0.375 to 0.375
- w_value: bfloat16 [256, 2048], P(None, 'head'), may hold values from -0.375 to 0.375
- w_out: bfloat16 [2048, 256], P('head'), may hold values from -0.125 to 0.125
- cotangent: bfloat16 [2, 4096, 256], P('dp', 'frame'), may hold values from -6 to 6
Outputs:
- grad_spatial: float32 [9, 256, 256], replicated
- grad_temporal: float32 [3, 256, 256], replicated
- grad_query: float32 [256, 2048], P(None, 'head')
- grad_key: float32 [256, 2048], P(None, 'head')
- grad_value: float32 [256, 2048], P(None, 'head')
- grad_out: float32 [2048, 256], P('head')
Inputs may be any that keep to these rules, and one draw needn't show every extreme that they name: `block_ids`: block numbers never fall along a clip's tokens; every block has 1 to (128) tokens.
All inputs are finite; a program needn't handle non-finite values.
Results may differ from a plain program's by a relative error of at most 0.04.
Values may be sent and summed in bfloat16 or wider, within the bound.
No kernel may reach another device: no remote copies, remote signals or barrier semaphores. Data moves between devices by JAX's collectives and lax.ppermute only.
A program may use at most 128 MiB of HBM per device.

v0:
```python
import jax
import jax.numpy as jnp
from jax import lax
from jax.sharding import PartitionSpec as P

HD = 128
SIDE = 8
NEG_FILL = -1e30


def with_halo(cells, sides, width):
    for axis, dim in sides:
        count = lax.axis_size(axis)
        ends = count - 1
        head = lax.slice_in_dim(cells, 0, width, axis=dim)
        tail = lax.slice_in_dim(cells, cells.shape[dim] - width, cells.shape[dim], axis=dim)
        cells = jnp.concatenate(
            [
                lax.ppermute(tail, axis, [(i, (i + 1) % count) for i in range(ends)]),
                cells,
                lax.ppermute(head, axis, [((i + 1) % count, i) for i in range(ends)]),
            ],
            axis=dim,
        )
    return cells


def spatial_taps(frame_grid, side):
    padded = jnp.pad(frame_grid, ((0, 0), (1, 1), (1, 1), (0, 0)))
    count = frame_grid.shape[0] * side * side
    width = frame_grid.shape[3]
    return [
        padded[:, row_off : row_off + side, col_off : col_off + side, :].reshape(count, width)
        for row_off in range(3)
        for col_off in range(3)
    ]


def silu_slope(pre_act):
    sigma = jax.nn.sigmoid(pre_act)
    return sigma * (1.0 + pre_act * (1.0 - sigma))


def frame_rims(field):
    return with_halo(field, (("frame", 0),), SIDE * SIDE)


def take_head(matrix, which_head):
    return matrix[:, which_head * HD : (which_head + 1) * HD]


def contract_rows(left, right):
    return lax.dot_general(
        left, right, (((0,), (0,)), ((), ())), preferred_element_type=jnp.float32
    )


def on_device(clip, block_ids, w_spatial, w_temporal, w_query, w_key, w_value, w_out, cotangent):
    frames_in = clip[0]
    upstream = cotangent[0]
    clip_blocks = block_ids[0]
    tok_local, channels = frames_in.shape
    frame_len = SIDE * SIDE
    scale = HD ** (-0.5)
    grid = frames_in.reshape(tok_local // frame_len, SIDE, SIDE, channels)
    taps = spatial_taps(grid, SIDE)
    pre_act = jnp.zeros((tok_local, channels), jnp.float32)
    for offset in range(9):
        pre_act = pre_act + jnp.dot(
            taps[offset], w_spatial[offset], preferred_element_type=jnp.float32
        )
    hidden = jax.nn.silu(pre_act).astype(jnp.bfloat16)
    hidden_rim = frame_rims(hidden)
    temporal = jnp.zeros((tok_local, channels), jnp.float32)
    for offset in range(3):
        temporal = temporal + jnp.dot(
            hidden_rim[offset * frame_len : offset * frame_len + tok_local],
            w_temporal[offset],
            preferred_element_type=jnp.float32,
        )
    features = temporal.astype(jnp.bfloat16)
    queries_local = jnp.dot(features, w_query, preferred_element_type=jnp.float32).astype(
        jnp.bfloat16
    )
    keys_local = jnp.dot(features, w_key, preferred_element_type=jnp.float32).astype(jnp.bfloat16)
    values_local = jnp.dot(features, w_value, preferred_element_type=jnp.float32).astype(
        jnp.bfloat16
    )
    keys_every, values_every = (
        lax.all_gather(keys_local, "frame", axis=0, tiled=True),
        lax.all_gather(values_local, "frame", axis=0, tiled=True),
    )
    first_row = lax.axis_index("frame") * tok_local
    grad_attended = jnp.dot(upstream, w_out.T, preferred_element_type=jnp.float32).astype(
        jnp.bfloat16
    )
    queries_held, grad_held = (queries_local, grad_attended)
    held_blocks = lax.dynamic_slice_in_dim(clip_blocks, first_row, tok_local)
    visible = clip_blocks[None, :] <= held_blocks[:, None]
    heads_here = queries_local.shape[1] // HD
    width_here = queries_local.shape[1]
    attended_parts, grad_query_parts, prob_list, score_grads, norm_list, delta_list = (
        [],
        [],
        [],
        [],
        [],
        [],
    )
    for which_head in range(heads_here):
        query_head = take_head(queries_held, which_head)
        key_head = take_head(keys_every, which_head)
        value_head = take_head(values_every, which_head)
        grad_head = take_head(grad_held, which_head)
        scores = jnp.dot(query_head, key_head.T, preferred_element_type=jnp.float32) * scale
        masked = jnp.where(visible, scores, NEG_FILL)
        top = jnp.max(masked, axis=1, keepdims=True)
        total = jnp.sum(jnp.where(visible, jnp.exp(masked - top), 0.0), axis=1, keepdims=True)
        log_norm = top + jnp.log(total)
        probs = jnp.where(visible, jnp.exp(masked - log_norm), 0.0)
        probs_low = probs.astype(jnp.bfloat16)
        attended = jnp.dot(probs_low, value_head, preferred_element_type=jnp.float32).astype(
            jnp.bfloat16
        )
        delta = jnp.sum(
            grad_head.astype(jnp.float32) * attended.astype(jnp.float32), axis=1, keepdims=True
        )
        grad_probs = jnp.dot(grad_head, value_head.T, preferred_element_type=jnp.float32)
        grad_scores = (probs * (grad_probs - delta) * scale).astype(jnp.bfloat16)
        grad_query_parts.append(
            jnp.dot(grad_scores, key_head, preferred_element_type=jnp.float32).astype(jnp.bfloat16)
        )
        attended_parts.append(attended)
        prob_list.append(probs_low)
        score_grads.append(grad_scores)
        norm_list.append(log_norm)
        delta_list.append(delta)
    attended_all = jnp.concatenate(attended_parts, axis=1)
    grad_queries = jnp.concatenate(grad_query_parts, axis=1)
    key_parts = []
    value_parts = []
    for which_head in range(heads_here):
        score_cols = score_grads[which_head]
        prob_cols = prob_list[which_head]
        key_parts.append(contract_rows(score_cols, take_head(queries_held, which_head)))
        value_parts.append(contract_rows(prob_cols, take_head(grad_held, which_head)))
    summed = lax.psum_scatter(
        jnp.concatenate(key_parts + value_parts, axis=1), "frame", scatter_dimension=0, tiled=True
    )
    grad_keys = summed[:, :width_here].astype(jnp.bfloat16)
    grad_values = summed[:, width_here:].astype(jnp.bfloat16)
    grad_wq_local = contract_rows(features, grad_queries)
    grad_wk_local = contract_rows(features, grad_keys)
    grad_wv_local = contract_rows(features, grad_values)
    grad_wo_local = contract_rows(attended_all, upstream)
    back_part = jnp.dot(grad_queries, w_query.T, preferred_element_type=jnp.float32)
    back_part = back_part + jnp.dot(grad_keys, w_key.T, preferred_element_type=jnp.float32)
    back_part = back_part + jnp.dot(grad_values, w_value.T, preferred_element_type=jnp.float32)
    head_sum = lax.psum(back_part, "head")
    grad_features = (head_sum + upstream.astype(jnp.float32)).astype(jnp.bfloat16)
    grad_rim = frame_rims(grad_features)
    grad_wt = jnp.stack(
        [
            contract_rows(
                hidden_rim[offset * frame_len : offset * frame_len + tok_local], grad_features
            )
            for offset in range(3)
        ]
    )
    grad_hidden = jnp.zeros((tok_local, channels), jnp.float32)
    for offset in range(3):
        grad_hidden = grad_hidden + jnp.dot(
            grad_rim[(2 - offset) * frame_len : (2 - offset) * frame_len + tok_local],
            w_temporal[offset].T,
            preferred_element_type=jnp.float32,
        )
    grad_pre = (grad_hidden * silu_slope(pre_act)).astype(jnp.bfloat16)
    grad_ws = jnp.stack([contract_rows(taps[offset], grad_pre) for offset in range(9)])
    totals = lax.psum(
        (grad_ws, grad_wt, grad_wq_local, grad_wk_local, grad_wv_local, grad_wo_local),
        ("frame", "dp"),
    )
    factor = float(lax.axis_size("dp") * lax.axis_size("frame") * tok_local) ** (-0.5)
    return (
        totals[0] * factor,
        totals[1] * factor,
        totals[2] * factor,
        totals[3] * factor,
        totals[4] * factor,
        totals[5] * factor,
    )


def solution(mesh):
    in_specs = (
        P("dp", "frame", None),
        P("dp", None),
        P(),
        P(),
        P(None, "head"),
        P(None, "head"),
        P(None, "head"),
        P("head", None),
        P("dp", "frame", None),
    )
    out_specs = (P(), P(), P(None, "head"), P(None, "head"), P(None, "head"), P("head", None))
    return jax.shard_map(
        on_device, mesh=mesh, in_specs=in_specs, out_specs=out_specs, check_vma=False
    )
```

profile of v0, /device:TPU:8, one launch (start us, length us, event | category | flops | bytes accessed | tf_op | source)
XLA Modules:
  0.0 700.0 jit_solution(11616659482293236148)
XLA Ops:
  7.2 1.9 pad_slice_fusion
  9.2 1.2 fusion.60
  10.4 1.1 convolution_add_fusion.11
  13.6 4.0 collective-permute-start
  17.6 1.3 collective-permute-start.1
  19.1 4.3 collective-permute-done.1
  24.8 1.7 convolution_convert_fusion
  27.7 85.4 %all-gather.3.cloned.1.call-done = bf16[4096,256]{1,0:T(8,128)(2,1)} async-done(((bf16[256,256]{1,0:T(8,128)(2,1)}), bf16[4096,256]{1,0:T(8,128)(2,1)}) %all-gather.3.cloned.1.call-update) | async-done | bytes 2097168 | tf_op jit(solution)/shard_map/all_gather | solution.py:90
  113.1 2.3 fusion.108
  116.3 1.9 fusion.6
  118.7 2.4 fusion.9
  121.1 1.3 copy-done.1
  122.4 1.8 fusion.91
  124.2 1.8 fusion.94
  126.0 72.5 %all-gather.5.cloned.1.call-done = bf16[4096,256]{1,0:T(8,128)(2,1)} async-done(((bf16[256,256]{1,0:T(8,128)(2,1)}), bf16[4096,256]{1,0:T(8,128)(2,1)}) %all-gather.5.cloned.1.call-update) | async-done | bytes 2097168 | tf_op jit(solution)/shard_map/all_gather | solution.py:91
  198.4 2.8 convolution_convert_fusion.5
  201.3 2.9 multiply_reduce_fusion.1
  204.3 1.7 fusion.5
  206.5 1.7 copy-done.4
  208.1 1.7 fusion.4
  209.8 1.3 copy-done.2
  211.6 1.1 copy-done.7
  213.4 3.8 pad_maximum_fusion
  217.4 2.8 convolution_convert_fusion.6
  223.3 216.4 %reduce-scatter.2.cloned.1.call-done = f32[256,512]{0,1:T(8,128)} async-done(((f32[4096,512]{0,1:T(8,128)}), f32[256,512]{0,1:T(8,128)}) %reduce-scatter.2.cloned.1.call-update) | async-done | bytes 524304 | tf_op jit(solution)/shard_map/reduce_scatter | solution.py:147
  439.7 1.1 convert.4
  443.9 60.5 %all-reduce.5.cloned.1.call-done = f32[256,256]{1,0:T(8,128)} async-done(((f32[256,256]{1,0:T(8,128)}), f32[256,256]{1,0:T(8,128)}) %all-reduce.5.cloned.1.call-update) | async-done | bytes 262160 | tf_op jit(solution)/shard_map/psum | solution.py:159
  505.8 1.3 collective-permute-start.2
  507.1 4.5 collective-permute-start.3
  515.8 1.4 copy-done.9
  517.3 168.9 %all-reduce.7.cloned.1.call-done = (f32[9,256,256]{2,1,0:T(8,128)}, f32[3,256,256]{2,1,0:T(8,128)}, f32[256,256]{1,0:T(8,128)}, f32[256,256]{1,0:T(8,128)}, f32[256,256]{1,0:T(8,128)}, /*index=5*/f32[256,256]{1,0:T(8,128)}) async-done(((f32[9,256,256]{2,1,0:T(8,128)}, f32[3,256,256]{2,1,0:T(8,128)}, f32[256,256]{1,0:T(8,128)}, f32[256,256]{1,0:T(8,128)}, f32[256,256]{1,0:T(8,128)}, ...) | async-done | bytes 4194320 | tf_op jit(solution)/shard_map/psum | solution.py:179
  686.1 3.4 broadcast_multiply_fusion
  (158 shorter events, 23.3 us)
Async XLA Ops:
  7.2 20.4 %copy-start = (bf16[256,256]{1,0:T(8,128)(2,1)S(1)}, bf16[256,256]{1,0:T(8,128)(2,1)}, u32[]{:S(2)}) copy-start(bf16[256,256]{1,0:T(8,128)(2,1)} %param.13) | copy-start | bytes 393220
  7.2 4.7 copy-start.14
  7.2 4.3 copy-start.19
  7.2 105.9 %all-gather.3.cloned.1.call-start = ((), (), s32[]{:S(2)}) async-start(), calls=%async_computation.1 | async-start | bytes 2228224 | tf_op jit(solution)/shard_map/all_gather | solution.py:90
  11.9 7.0 %copy-start.17 = (bf16[3,256,256]{2,1,0:T(8,128)(2,1)S(1)}, bf16[3,256,256]{2,1,0:T(8,128)(2,1)}, u32[]{:S(2)}) copy-start(bf16[3,256,256]{2,1,0:T(8,128)(2,1)} %param.12) | copy-start | bytes 1179652
  12.5 11.3 %copy-start.27 = (bf16[256,256]{1,0:T(8,128)(2,1)S(1)}, bf16[256,256]{1,0:T(8,128)(2,1)}, u32[]{:S(2)}) copy-start(bf16[256,256]{1,0:T(8,128)(2,1)} %param.14) | copy-start | bytes 393220
  12.7 13.9 %copy-start.42 = (s32[1,4096]{1,0:T(1,128)S(1)}, s32[1,4096]{1,0:T(1,128)}, u32[]{:S(2)}) copy-start(s32[1,4096]{1,0:T(1,128)} %param.10) | copy-start | bytes 49156
  12.7 13.9 %copy-start.13 = (bf16[1,256,256]{2,1,0:T(8,128)(2,1)S(1)}, bf16[1,256,256]{2,1,0:T(8,128)(2,1)}, u32[]{:S(2)}) copy-start(bf16[1,256,256]{2,1,0:T(8,128)(2,1)} %param.17) | copy-start | bytes 393220
  13.6 13.0 %copy-start.37 = (bf16[256,256]{1,0:T(8,128)(2,1)S(1)}, bf16[256,256]{1,0:T(8,128)(2,1)}, u32[]{:S(2)}) copy-start(bf16[256,256]{1,0:T(8,128)(2,1)} %param.16) | copy-start | bytes 393220
  13.6 10.0 %collective-permute-start = (bf16[64,256]{1,0:T(8,128)(2,1)S(1)}, bf16[64,256]{1,0:T(8,128)(2,1)S(1)}, u32[]{:S(2)}, u32[]{:S(2)}) collective-permute-start(bf16[64,256]{1,0:T(8,128)(2,1)S(1)} %get-tuple-element.18), channel_id=1, source_target_pairs={{0,16},{16,32},{32,48},{48,64},{64,80},{80,96},{96,112},{112,128},... | collective-permute-start | bytes 98312 | tf_op jit(solution)/shard_map/ppermute | solution.py:19
  17.6 5.8 collective-permute-start.1
  23.4 91.9 %copy-start.38 = (bf16[64,256]{1,0:T(8,128)(2,1)}, bf16[64,256]{1,0:T(8,128)(2,1)S(1)}, u32[]{:S(2)}) copy-start(bf16[64,256]{1,0:T(8,128)(2,1)S(1)} %collective-permute-done.1) | copy-start | bytes 98308
  23.6 91.7 %copy-start.40 = (bf16[64,256]{1,0:T(8,128)(2,1)}, bf16[64,256]{1,0:T(8,128)(2,1)S(1)}, u32[]{:S(2)}) copy-start(bf16[64,256]{1,0:T(8,128)(2,1)S(1)} %collective-permute-done) | copy-start | bytes 98308
  24.7 173.7 %all-gather.5.cloned.1.call-start = ((), (), s32[]{:S(2)}) async-start(), calls=%async_computation.2 | async-start | bytes 2228224 | tf_op jit(solution)/shard_map/all_gather | solution.py:91
  26.5 413.2 %reduce-scatter.2.cloned.1.call-start = ((), (), s32[]{:S(2)}) async-start(), calls=%async_computation.3 | async-start | bytes 8912896 | tf_op jit(solution)/shard_map/reduce_scatter | solution.py:147
  26.6 89.7 %copy-start.43 = (s32[1,256]{1,0:T(1,128)}, s32[1,256]{1,0:T(1,128)S(1)}, u32[]{:S(2)}) copy-start(s32[1,256]{1,0:T(1,128)S(1)} %constant_dynamic-slice_fusion) | copy-start | bytes 3076
  27.7 87.6 %copy-start.25 = (bf16[256,256]{1,0:T(8,128)(2,1)}, bf16[256,256]{1,0:T(8,128)(2,1)S(1)}, u32[]{:S(2)}) copy-start(bf16[256,256]{1,0:T(8,128)(2,1)S(1)} %convolution_convert_fusion.3) | copy-start | bytes 393220
  198.4 5.8 copy-start.6
  201.3 4.7 copy-start.23
  217.2 287.1 %all-reduce.5.cloned.1.call-start = ((), (), s32[]{:S(2)}) async-start(), calls=%async_computation.4 | async-start | bytes 524288 | tf_op jit(solution)/shard_map/psum | solution.py:159
  221.2 220.5 %copy-start.28 = (bf16[256,256]{1,0:T(8,128)(2,1)S(1)}, bf16[256,256]{1,0:T(8,128)(2,1)}, u32[]{:S(2)}) copy-start(bf16[256,256]{1,0:T(8,128)(2,1)} %param.14) | copy-start | bytes 393220
  221.2 220.8 %copy-start.29 = (bf16[256,256]{1,0:T(8,128)(2,1)S(1)}, bf16[256,256]{1,0:T(8,128)(2,1)}, u32[]{:S(2)}) copy-start(bf16[256,256]{1,0:T(8,128)(2,1)} %param.15) | copy-start | bytes 393220
  223.3 282.3 %copy-start.18 = (bf16[3,256,256]{2,1,0:T(8,128)(2,1)S(1)}, bf16[3,256,256]{2,1,0:T(8,128)(2,1)}, u32[]{:S(2)}) copy-start(bf16[3,256,256]{2,1,0:T(8,128)(2,1)} %param.12) | copy-start | bytes 1179652
  440.8 70.9 %copy-start.41 = (bf16[64,256]{1,0:T(8,128)(2,1)S(1)}, bf16[64,256]{1,0:T(8,128)(2,1)}, u32[]{:S(2)}) copy-start(bf16[64,256]{1,0:T(8,128)(2,1)} %copy-done.40) | copy-start | bytes 98308
  441.7 70.2 %copy-start.39 = (bf16[64,256]{1,0:T(8,128)(2,1)S(1)}, bf16[64,256]{1,0:T(8,128)(2,1)}, u32[]{:S(2)}) copy-start(bf16[64,256]{1,0:T(8,128)(2,1)} %copy-done.38) | copy-start | bytes 98308
  442.9 243.2 %all-reduce.7.cloned.1.call-start = ((), (), s32[]{:S(2)}) async-start(), calls=%async_computation.5 | async-start | bytes 8388608 | tf_op jit(solution)/shard_map/psum | solution.py:179
  443.9 69.6 %copy-start.49 = (f32[256,256]{1,0:T(8,128)S(1)}, f32[256,256]{1,0:T(8,128)}, u32[]{:S(2)}) copy-start(f32[256,256]{1,0:T(8,128)} %get-tuple-element.31) | copy-start | bytes 786436
  505.8 7.7 %collective-permute-start.2 = (bf16[64,256]{1,0:T(8,128)(2,1)S(1)}, bf16[64,256]{1,0:T(8,128)(2,1)S(1)}, u32[]{:S(2)}, u32[]{:S(2)}) collective-permute-start(bf16[64,256]{1,0:T(8,128)(2,1)S(1)} %get-tuple-element.16), channel_id=1, source_target_pairs={{16,0},{32,16},{48,32},{64,48},{80,64},{96,80},{112,96},{128,112},... | collective-permute-start | bytes 98312 | tf_op jit(solution)/shard_map/ppermute | solution.py:21
  507.1 6.1 collective-permute-start.3
  686.1 4.9 copy-start.33
  686.1 5.6 copy-start.32
  686.1 6.3 copy-start.22
  (27 other events, 67.7 us)
Sparse Core Ops, SparseCore 0:
  24.8 88.2 all-gather.2
  116.2 82.1 all-gather.4
  217.3 222.3 reduce-scatter.1
  443.1 61.2 all-reduce.4
  517.4 168.7 all-reduce.6
where the time goes:
time: 700 us
  waiting for transfers between devices  608 us (87%)
  matrix products  37.3 us (5%)
  other arithmetic  18.4 us (3%)
  between operations  14.7 us (2%)
  starting transfers between devices  11.5 us (2%)
  local copies, waits for them, and re-layouts  9.96 us (1%)
    reduce_scatter x1, waiting for transfers between devices, on_device(): lax.psum_scatter(jnp.concatenate(key_parts + value_parts, axis=1), 'frame...  216 us
    psum x1, waiting for transfers between devices, on_device(): lax.psum((grad_ws, grad_wt, grad_wq_local, grad_wk_local, grad_wv_local,...  169 us
    all_gather x1, waiting for transfers between devices, on_device(): lax.all_gather(keys_local, 'frame', axis=0, tiled=True)  85.4 us
    all_gather x1, waiting for transfers between devices, on_device(): lax.all_gather(values_local, 'frame', axis=0, tiled=True)  72.5 us
    psum x1, waiting for transfers between devices, on_device(): head_sum = lax.psum(back_part, 'head')  60.5 us
  transfers between devices with their start and end apart: 9, of which 7 were waited for; matrix products, arithmetic and copies ran while one was open for 3% of the time, Pallas kernels for 0%

commit v1 on v0

--- a/solution.py
+++ b/solution.py
@@ -6,6 +6,11 @@
 HD = 128
 SIDE = 8
 NEG_FILL = -1e30
+
+
+def by_each_axis(array, one, other):
+    partial = lax.psum(array, one)
+    return lax.psum(partial, other)
 
 
 def with_halo(cells, sides, width):
@@ -176,9 +181,10 @@
         )
     grad_pre = (grad_hidden * silu_slope(pre_act)).astype(jnp.bfloat16)
     grad_ws = jnp.stack([contract_rows(taps[offset], grad_pre) for offset in range(9)])
-    totals = lax.psum(
+    totals = by_each_axis(
         (grad_ws, grad_wt, grad_wq_local, grad_wk_local, grad_wv_local, grad_wo_local),
-        ("frame", "dp"),
+        "dp",
+        "frame",
     )
     factor = float(lax.axis_size("dp") * lax.axis_size("frame") * tok_local) ** (-0.5)
     return (

time: 700 us -> 835 us (1.19)
  waiting for transfers between devices: 608 us -> 743 us
    psum x1 -> x2, waiting for transfers between devices: 169 us -> 303 us  [the longest x1 178 us: by_each_axis(): return lax.psum(partial, other)]
  transfers between devices with their start and end apart: 9 -> 10, of which waited for: 7 -> 8; matrix products, arithmetic and copies ran while one was open for 3% -> 3% of each run, Pallas kernels for 0% -> 0%
where the time goes in v1:
time: 835 us
  waiting for transfers between devices  743 us (89%)
  matrix products  37.3 us (4%)
  other arithmetic  18.4 us (2%)
  between operations  15 us (2%)
  starting transfers between devices  11.5 us (1%)
  local copies, waits for them, and re-layouts  10.2 us (1%)
    reduce_scatter x1, waiting for transfers between devices, on_device(): lax.psum_scatter(jnp.concatenate(key_parts + value_parts, axis=1), 'frame...  217 us
    psum x1, waiting for transfers between devices, by_each_axis(): return lax.psum(partial, other)  178 us
    psum x1, waiting for transfers between devices, by_each_axis(): partial = lax.psum(array, one)  125 us
    all_gather x1, waiting for transfers between devices, on_device(): lax.all_gather(keys_local, 'frame', axis=0, tiled=True)  85.4 us
    all_gather x1, waiting for transfers between devices, on_device(): lax.all_gather(values_local, 'frame', axis=0, tiled=True)  72.5 us
    psum x1, waiting for transfers between devices, on_device(): head_sum = lax.psum(back_part, 'head')  60.3 us
  transfers between devices with their start and end apart: 10, of which 8 were waited for; matrix products, arithmetic and copies ran while one was open for 3% of the time, Pallas kernels for 0%

profile of v1, /device:TPU:8, one launch (start us, length us, event | category | flops | bytes accessed | tf_op | source)
XLA Modules:
  0.0 835.1 jit_solution(9086440338307810512)
XLA Ops:
  7.2 1.7 pad_slice_fusion
  9.0 1.2 fusion.60
  10.2 1.1 convolution_add_fusion.11
  13.4 3.9 collective-permute-start
  17.4 1.3 collective-permute-start.1
  18.9 4.3 collective-permute-done.1
  24.9 1.8 convolution_convert_fusion
  27.9 85.4 %all-gather.3.cloned.1.call-done = bf16[4096,256]{1,0:T(8,128)(2,1)} async-done(((bf16[256,256]{1,0:T(8,128)(2,1)}), bf16[4096,256]{1,0:T(8,128)(2,1)}) %all-gather.3.cloned.1.call-update) | async-done | bytes 2097168 | tf_op jit(solution)/shard_map/all_gather | solution.py:95
  113.3 2.3 fusion.108
  116.5 1.9 fusion.6
  118.9 2.4 fusion.9
  121.3 1.3 copy-done.1
  122.6 1.7 fusion.91
  124.4 1.8 fusion.94
  126.1 72.5 %all-gather.5.cloned.1.call-done = bf16[4096,256]{1,0:T(8,128)(2,1)} async-done(((bf16[256,256]{1,0:T(8,128)(2,1)}), bf16[4096,256]{1,0:T(8,128)(2,1)}) %all-gather.5.cloned.1.call-update) | async-done | bytes 2097168 | tf_op jit(solution)/shard_map/all_gather | solution.py:96
  198.6 2.8 convolution_convert_fusion.5
  201.5 2.9 multiply_reduce_fusion.1
  204.5 1.7 fusion.5
  206.7 1.7 copy-done.4
  208.3 1.7 fusion.4
  210.0 1.3 copy-done.2
  211.8 1.1 copy-done.7
  213.6 3.8 pad_maximum_fusion
  217.7 2.8 convolution_convert_fusion.6
  223.5 216.6 %reduce-scatter.2.cloned.1.call-done = f32[256,512]{0,1:T(8,128)} async-done(((f32[4096,512]{0,1:T(8,128)}), f32[256,512]{0,1:T(8,128)}) %reduce-scatter.2.cloned.1.call-update) | async-done | bytes 524304 | tf_op jit(solution)/shard_map/reduce_scatter | solution.py:152
  444.3 60.3 %all-reduce.7.cloned.1.call-done = f32[256,256]{1,0:T(8,128)} async-done(((f32[256,256]{1,0:T(8,128)}), f32[256,256]{1,0:T(8,128)}) %all-reduce.7.cloned.1.call-update) | async-done | bytes 262160 | tf_op jit(solution)/shard_map/psum | solution.py:164
  506.0 1.3 collective-permute-start.2
  507.3 4.5 collective-permute-start.3
  516.0 1.4 copy-done.9
  517.5 125.2 %all-reduce.11.cloned.1.call-done = (f32[9,256,256]{2,1,0:T(8,128)}, f32[3,256,256]{2,1,0:T(8,128)}, f32[256,256]{1,0:T(8,128)}, f32[256,256]{1,0:T(8,128)}, f32[256,256]{1,0:T(8,128)}, /*index=5*/f32[256,256]{1,0:T(8,128)}) async-done(((f32[9,256,256]{2,1,0:T(8,128)}, f32[3,256,256]{2,1,0:T(8,128)}, f32[256,256]{1,0:T(8,128)}, f32[256,256]{1,0:T(8,128)}, f32[256,256]{1,0:T(8,128)}, ...) | async-done | bytes 4194320 | tf_op jit(solution)/shard_map/psum | solution.py:12
  642.7 178.2 %all-reduce.9.cloned.1.call-done = (f32[9,256,256]{2,1,0:T(8,128)}, f32[3,256,256]{2,1,0:T(8,128)}, f32[256,256]{1,0:T(8,128)}, f32[256,256]{1,0:T(8,128)}, f32[256,256]{1,0:T(8,128)}, /*index=5*/f32[256,256]{1,0:T(8,128)}) async-done(((f32[9,256,256]{2,1,0:T(8,128)}, f32[3,256,256]{2,1,0:T(8,128)}, f32[256,256]{1,0:T(8,128)}, f32[256,256]{1,0:T(8,128)}, f32[256,256]{1,0:T(8,128)}, ...) | async-done | bytes 4194320 | tf_op jit(solution)/shard_map/psum | solution.py:13
  820.9 3.4 broadcast_multiply_fusion
  (161 shorter events, 24.9 us)
Async XLA Ops:
  7.2 20.5 %copy-start = (bf16[256,256]{1,0:T(8,128)(2,1)S(1)}, bf16[256,256]{1,0:T(8,128)(2,1)}, u32[]{:S(2)}) copy-start(bf16[256,256]{1,0:T(8,128)(2,1)} %param.13) | copy-start | bytes 393220
  7.2 4.5 copy-start.14
  7.2 106.1 %all-gather.3.cloned.1.call-start = ((), (), s32[]{:S(2)}) async-start(), calls=%async_computation.1 | async-start | bytes 2228224 | tf_op jit(solution)/shard_map/all_gather | solution.py:95
  11.7 7.0 copy-start.17
  12.3 11.7 %copy-start.27 = (bf16[256,256]{1,0:T(8,128)(2,1)S(1)}, bf16[256,256]{1,0:T(8,128)(2,1)}, u32[]{:S(2)}) copy-start(bf16[256,256]{1,0:T(8,128)(2,1)} %param.14) | copy-start | bytes 393220
  12.5 14.3 %copy-start.42 = (s32[1,4096]{1,0:T(1,128)S(1)}, s32[1,4096]{1,0:T(1,128)}, u32[]{:S(2)}) copy-start(s32[1,4096]{1,0:T(1,128)} %param.10) | copy-start | bytes 49156
  12.5 14.3 %copy-start.13 = (bf16[1,256,256]{2,1,0:T(8,128)(2,1)S(1)}, bf16[1,256,256]{2,1,0:T(8,128)(2,1)}, u32[]{:S(2)}) copy-start(bf16[1,256,256]{2,1,0:T(8,128)(2,1)} %param.17) | copy-start | bytes 393220
  13.4 13.4 %copy-start.37 = (bf16[256,256]{1,0:T(8,128)(2,1)S(1)}, bf16[256,256]{1,0:T(8,128)(2,1)}, u32[]{:S(2)}) copy-start(bf16[256,256]{1,0:T(8,128)(2,1)} %param.16) | copy-start | bytes 393220
  13.4 10.4 %collective-permute-start = (bf16[64,256]{1,0:T(8,128)(2,1)S(1)}, bf16[64,256]{1,0:T(8,128)(2,1)S(1)}, u32[]{:S(2)}, u32[]{:S(2)}) collective-permute-start(bf16[64,256]{1,0:T(8,128)(2,1)S(1)} %get-tuple-element.24), channel_id=1, source_target_pairs={{0,16},{16,32},{32,48},{48,64},{64,80},{80,96},{96,112},{112,128},... | collective-permute-start | bytes 98312 | tf_op jit(solution)/shard_map/ppermute | solution.py:24
  17.4 5.8 collective-permute-start.1
  23.8 91.7 %copy-start.40 = (bf16[64,256]{1,0:T(8,128)(2,1)}, bf16[64,256]{1,0:T(8,128)(2,1)S(1)}, u32[]{:S(2)}) copy-start(bf16[64,256]{1,0:T(8,128)(2,1)S(1)} %collective-permute-done) | copy-start | bytes 98308
  24.9 173.7 %all-gather.5.cloned.1.call-start = ((), (), s32[]{:S(2)}) async-start(), calls=%async_computation.2 | async-start | bytes 2228224 | tf_op jit(solution)/shard_map/all_gather | solution.py:96
  26.7 413.3 %reduce-scatter.2.cloned.1.call-start = ((), (), s32[]{:S(2)}) async-start(), calls=%async_computation.3 | async-start | bytes 8912896 | tf_op jit(solution)/shard_map/reduce_scatter | solution.py:152
  26.8 89.7 %copy-start.43 = (s32[1,256]{1,0:T(1,128)}, s32[1,256]{1,0:T(1,128)S(1)}, u32[]{:S(2)}) copy-start(s32[1,256]{1,0:T(1,128)S(1)} %constant_dynamic-slice_fusion) | copy-start | bytes 3076
  27.9 87.7 %copy-start.25 = (bf16[256,256]{1,0:T(8,128)(2,1)}, bf16[256,256]{1,0:T(8,128)(2,1)S(1)}, u32[]{:S(2)}) copy-start(bf16[256,256]{1,0:T(8,128)(2,1)S(1)} %convolution_convert_fusion.3) | copy-start | bytes 393220
  198.6 5.8 copy-start.6
  201.5 4.7 copy-start.23
  217.4 287.1 %all-reduce.7.cloned.1.call-start = ((), (), s32[]{:S(2)}) async-start(), calls=%async_computation.4 | async-start | bytes 524288 | tf_op jit(solution)/shard_map/psum | solution.py:164
  221.4 220.7 %copy-start.28 = (bf16[256,256]{1,0:T(8,128)(2,1)S(1)}, bf16[256,256]{1,0:T(8,128)(2,1)}, u32[]{:S(2)}) copy-start(bf16[256,256]{1,0:T(8,128)(2,1)} %param.14) | copy-start | bytes 393220
  221.4 220.9 %copy-start.29 = (bf16[256,256]{1,0:T(8,128)(2,1)S(1)}, bf16[256,256]{1,0:T(8,128)(2,1)}, u32[]{:S(2)}) copy-start(bf16[256,256]{1,0:T(8,128)(2,1)} %param.15) | copy-start | bytes 393220
  223.5 282.3 %copy-start.18 = (bf16[3,256,256]{2,1,0:T(8,128)(2,1)S(1)}, bf16[3,256,256]{2,1,0:T(8,128)(2,1)}, u32[]{:S(2)}) copy-start(bf16[3,256,256]{2,1,0:T(8,128)(2,1)} %param.12) | copy-start | bytes 1179652
  441.1 70.7 %copy-start.41 = (bf16[64,256]{1,0:T(8,128)(2,1)S(1)}, bf16[64,256]{1,0:T(8,128)(2,1)}, u32[]{:S(2)}) copy-start(bf16[64,256]{1,0:T(8,128)(2,1)} %copy-done.40) | copy-start | bytes 98308
  442.1 70.0 %copy-start.39 = (bf16[64,256]{1,0:T(8,128)(2,1)S(1)}, bf16[64,256]{1,0:T(8,128)(2,1)}, u32[]{:S(2)}) copy-start(bf16[64,256]{1,0:T(8,128)(2,1)} %copy-done.38) | copy-start | bytes 98308
  443.3 199.4 %all-reduce.11.cloned.1.call-start = ((), (), s32[]{:S(2)}) async-start(), calls=%async_computation.6 | async-start | bytes 8388608 | tf_op jit(solution)/shard_map/psum | solution.py:12
  444.3 69.4 %copy-start.49 = (f32[256,256]{1,0:T(8,128)S(1)}, f32[256,256]{1,0:T(8,128)}, u32[]{:S(2)}) copy-start(f32[256,256]{1,0:T(8,128)} %get-tuple-element.37) | copy-start | bytes 786436
  506.0 7.7 collective-permute-start.2
  507.3 6.1 collective-permute-start.3
  517.5 303.5 %all-reduce.9.cloned.1.call-start = ((), (), s32[]{:S(2)}) async-start(), calls=%async_computation.5 | async-start | bytes 8388608 | tf_op jit(solution)/shard_map/psum | solution.py:13
  820.9 4.2 copy-start.34
  820.9 4.9 copy-start.33
  820.9 5.6 copy-start.32
  820.9 6.3 copy-start.22
  (28 other events, 68.3 us)
Sparse Core Ops, SparseCore 0:
  25.0 88.2 all-gather.2
  116.4 82.1 all-gather.4
  217.5 222.4 reduce-scatter.1
  443.4 61.0 all-reduce.6
  517.6 125.0 all-reduce.10
  645.6 175.2 all-reduce.8
